TPU v7x, 128 devices: a whole 4x4x4 slice. The times are simulated.
128 devices in a mesh: tm: 16 (over y, x), orb: 8 (over z, core).
Axes of the slice: x: 4, y: 4, z: 4, core: 2. Of those that a mesh axis runs over, the one named last changes fastest.
Arguments:
- forward: bfloat16 [2, 2, 512, 128, 128], P(None, None, 'tm'), may hold values from -2 to 2
- backward_slab: bfloat16 [2, 2, 512, 128, 128], P(None, None, 'tm', 'orb'), may hold values from -2 to 2
- slot_time: int32 [512], replicated, may hold values from 0 to 511, as said below
- pattern: int32 [128, 128], replicated, may hold values 0 or 1
- coupling: float32 [128, 128], replicated, may hold values from -1 to 1
- hamiltonian: float32 [128, 128], replicated, may hold values from -0.8 to 0.8
- lesser_now: float32 [2, 128, 128], replicated, may hold values from -1.5 to 1.5
Outputs:
- lesser_next: float32 [2, 128, 128], P(None, 'orb')
Inputs may be any that keep to these rules, and one draw needn't show every extreme that they name: slot_time is a permutation of the 512 history times. The 32 slots of each index d of tm hold exactly 32 // 16 times of the range [e * 32, (e + 1) * 32) for every index e of tm.
All inputs are finite; a program needn't handle non-finite values.
Results may differ from a plain program's by a relative error of at most 0.0054.
Values may be sent and summed in bfloat16 or wider, within the bound.
No kernel may reach another device: no remote copies, remote signals or barrier semaphores. Data moves between devices by JAX's collectives and lax.ppermute only.
A program may use at most 64 MiB of HBM per device.

v0:
```python
import math
import jax
import jax.numpy as jnp
from jax import lax
from jax.sharding import PartitionSpec as P

history_step = 0.02
update_step = 0.5


def complex_einsum(form, left_re, left_im, right_re, right_im):
    real_part = jnp.einsum(
        form, left_re, right_re, preferred_element_type=jnp.float32
    ) - jnp.einsum(form, left_im, right_im, preferred_element_type=jnp.float32)
    imag_part = jnp.einsum(
        form, left_re, right_im, preferred_element_type=jnp.float32
    ) + jnp.einsum(form, left_im, right_re, preferred_element_type=jnp.float32)
    return (real_part, imag_part)


def self_energy(fwd_re, fwd_im, back_re, back_im, interaction, inter_rows, row_start, row_count):
    rows_re = lax.dynamic_slice_in_dim(fwd_re, row_start, row_count, 1)
    rows_im = lax.dynamic_slice_in_dim(fwd_im, row_start, row_count, 1)
    fwd_re32 = fwd_re.astype(jnp.float32)
    fwd_im32 = fwd_im.astype(jnp.float32)
    trans_re = jnp.swapaxes(back_re, 1, 2).astype(jnp.float32)
    trans_im = jnp.swapaxes(back_im, 1, 2).astype(jnp.float32)
    bubble_re = (fwd_re32 * trans_re - fwd_im32 * trans_im).astype(jnp.bfloat16)
    bubble_im = (fwd_re32 * trans_im + fwd_im32 * trans_re).astype(jnp.bfloat16)
    left_re = jnp.einsum(
        "ik,skj->sij", inter_rows, bubble_re, preferred_element_type=jnp.float32
    ).astype(jnp.bfloat16)
    left_im = jnp.einsum(
        "ik,skj->sij", inter_rows, bubble_im, preferred_element_type=jnp.float32
    ).astype(jnp.bfloat16)
    screen_re = jnp.einsum("sik,kj->sij", left_re, interaction, preferred_element_type=jnp.float32)
    screen_im = jnp.einsum("sik,kj->sij", left_im, interaction, preferred_element_type=jnp.float32)
    rows_re32 = rows_re.astype(jnp.float32)
    rows_im32 = rows_im.astype(jnp.float32)
    direct_re = rows_re32 * screen_re - rows_im32 * screen_im
    direct_im = rows_re32 * screen_im + rows_im32 * screen_re
    inter_rows32 = inter_rows.astype(jnp.float32)
    scaled_re = (inter_rows32[None, :, :, None] * fwd_re32[:, None]).astype(jnp.bfloat16)
    scaled_im = (inter_rows32[None, :, :, None] * fwd_im32[:, None]).astype(jnp.bfloat16)
    inner_re, inner_im = complex_einsum("slm,simj->silj", back_re, back_im, scaled_re, scaled_im)
    inter32 = interaction.astype(jnp.float32)
    weighted_re = (inner_re * inter32).astype(jnp.bfloat16)
    weighted_im = (inner_im * inter32).astype(jnp.bfloat16)
    exch_re, exch_im = complex_einsum("sil,silj->sij", rows_re, rows_im, weighted_re, weighted_im)
    sigma_re = (direct_re - exch_re).astype(jnp.bfloat16)
    sigma_im = (direct_im - exch_im).astype(jnp.bfloat16)
    return (sigma_re, sigma_im)


def block_terms(fwd_block, back_block, weights, interaction, inter_rows, row_start, row_count):
    summed = None
    scale = weights[:, None, None]
    for branch in (0, 1):
        other = 1 - branch
        factor = 1.0 if branch == 0 else -1.0
        sigma_re, sigma_im = self_energy(
            fwd_block[branch, 0],
            fwd_block[branch, 1],
            back_block[other, 0],
            back_block[other, 1],
            interaction,
            inter_rows,
            row_start,
            row_count,
        )
        prod_re, prod_im = complex_einsum(
            "sil,slj->sij", sigma_re, sigma_im, back_block[other, 0], back_block[other, 1]
        )
        term = factor * jnp.stack(
            [jnp.sum(scale * prod_re, axis=0), jnp.sum(scale * prod_im, axis=0)]
        )
        summed = term if summed is None else summed + term
    return summed


def history_terms(fwd_part, back_part, weights, interaction, inter_rows, row_start, row_count):
    slices_here = fwd_part.shape[2]
    block_size = math.gcd(max(4, 128 // row_count), slices_here)
    block_count = slices_here // block_size
    orbitals = fwd_part.shape[3]

    def add_block(block, running):
        start = block * block_size
        fwd_block = lax.dynamic_slice_in_dim(fwd_part, start, block_size, 2)
        back_block = lax.dynamic_slice_in_dim(back_part, start, block_size, 2)
        weight_block = lax.dynamic_slice_in_dim(weights, start, block_size, 0)
        return running + block_terms(
            fwd_block, back_block, weight_block, interaction, inter_rows, row_start, row_count
        )

    initial = jnp.zeros((2, row_count, orbitals), jnp.float32)
    return lax.fori_loop(0, block_count, add_block, initial)


def on_device(forward, backward_slab, slot_time, pattern, coupling, hamiltonian, lesser_now):
    tm_count = lax.axis_size("tm")
    my_time = lax.axis_index("tm")
    my_orb = lax.axis_index("orb")
    per_device = forward.shape[2]
    row_count = backward_slab.shape[3]
    per_peer = per_device // tm_count
    slices_all = per_device * tm_count
    row_start = my_orb * row_count
    time_start = my_time * per_device
    holder_of = slot_time // per_device
    my_holders = lax.dynamic_slice_in_dim(holder_of, time_start, per_device)
    send_order = jnp.argsort(my_holders, stable=True)
    sorted_slab = jnp.take(backward_slab, send_order, axis=2)
    holder_grid = holder_of.reshape(tm_count, per_device)
    time_grid = slot_time.reshape(tm_count, per_device)
    not_mine = (holder_grid != my_time).astype(jnp.int32)
    positions = jnp.argsort(not_mine, axis=1, stable=True)[:, :per_peer]
    times_here = jnp.take_along_axis(time_grid, positions, axis=1).reshape(per_device)
    natural = jnp.argsort(times_here - time_start)
    masked = coupling * pattern.astype(jnp.float32)
    interaction = ((masked + masked.T) * 0.5).astype(jnp.bfloat16)
    inter_rows = lax.dynamic_slice_in_dim(interaction, row_start, row_count, 0)
    time_index = time_start + jnp.arange(per_device, dtype=jnp.int32)
    edges = (time_index == 0) | (time_index == slices_all - 1)
    weights = jnp.where(edges, jnp.float32(0.5), jnp.float32(1.0)) * history_step
    full_sorted = lax.all_gather(sorted_slab, "orb", axis=3, tiled=True)
    arrived = lax.all_to_all(full_sorted, "tm", split_axis=2, concat_axis=2, tiled=True)
    back_full = jnp.take(arrived, natural, axis=2)
    local_collision = history_terms(
        forward, back_full, weights, interaction, inter_rows, row_start, row_count
    )
    summed_rows = lax.psum(local_collision, "tm")
    collision = lax.all_gather(summed_rows, "orb", axis=1, tiled=True)
    own_rows = lax.dynamic_slice_in_dim(collision, row_start, row_count, 1)
    own_columns = lax.dynamic_slice_in_dim(collision, row_start, row_count, 2)
    herm_re = own_rows[0] + own_columns[0].T
    herm_im = own_rows[1] - own_columns[1].T
    high = lax.Precision.HIGHEST
    ham_rows = lax.dynamic_slice_in_dim(hamiltonian, row_start, row_count, 0)
    lesser_rows = lax.dynamic_slice_in_dim(lesser_now, row_start, row_count, 1)
    comm_re = jnp.dot(ham_rows, lesser_now[0], precision=high) - jnp.dot(
        lesser_rows[0], hamiltonian, precision=high
    )
    comm_im = jnp.dot(ham_rows, lesser_now[1], precision=high) - jnp.dot(
        lesser_rows[1], hamiltonian, precision=high
    )
    next_re = lesser_rows[0] + update_step * (comm_im + herm_im)
    next_im = lesser_rows[1] - update_step * (comm_re + herm_re)
    return jnp.stack([next_re, next_im])


def solution(mesh):
    in_specs = (
        P(None, None, "tm", None, None),
        P(None, None, "tm", "orb", None),
        P(),
        P(),
        P(),
        P(),
        P(),
    )
    out_specs = P(None, "orb", None)
    return jax.shard_map(
        on_device, mesh=mesh, in_specs=in_specs, out_specs=out_specs, check_vma=False
    )
```

profile of v0, /device:TPU:1, one launch (start us, length us, event | category | flops | bytes accessed | tf_op | source)
XLA Modules:
  0.0 479.0 jit_solution(11907473625283810762)
XLA Ops:
  10.6 39.5 %all-gather.2.cloned.1.call-done = bf16[2,2,32,128,128]{4,3,1,0,2:T(8,128)(2,1)} async-done(((bf16[2,2,32,16,128]{4,3,1,0,2:T(8,128)(2,1)}), bf16[2,2,32,128,128]{4,3,1,0,2:T(8,128)(2,1)}) %all-gather.2.cloned.1.call-update) | async-done | bytes 4194320 | tf_op jit(solution)/shard_map/all_gather | solution.py:126
  50.1 6.6 %all-to-all-start = ((bf16[2,2,32,128,128]{4,3,1,0,2:T(8,128)(2,1)}), bf16[2,2,32,128,128]{4,3,1,0,2:T(8,128)(2,1)}, u32[]{:S(2)}, u32[]{:S(2)}) async-start(bf16[2,2,32,128,128]{4,3,1,0,2:T(8,128)(2,1)} %all-gather.2.cloned.1.call-done), calls=%async_computation | async-start | bytes 8388608 | tf_op jit(solution)/shard_map/all_to_all | solution.py:127
  64.0 55.6 %all-to-all-done = bf16[2,2,32,128,128]{4,3,1,0,2:T(8,128)(2,1)} async-done(((bf16[2,2,32,128,128]{4,3,1,0,2:T(8,128)(2,1)}), bf16[2,2,32,128,128]{4,3,1,0,2:T(8,128)(2,1)}, u32[]{:S(2)}, u32[]{:S(2)}) %all-to-all-start) | async-done | bytes 4194336 | tf_op jit(solution)/shard_map/all_to_all | solution.py:127
  119.6 4.7 copy.45
  124.3 5.2 %gather_fusion.1 = bf16[32,2,2,128,128]{4,3,2,1,0:T(8,128)(2,1)} fusion(bf16[2,2,32,128,128]{4,3,2,1,0:T(8,128)(2,1)} %copy.45, s32[1024]{0:T(1024)S(1)} %pad_clamp_fusion), kind=kCustom, calls=%fused_computation.1 | custom fusion | bytes 8388736 | tf_op jit(solution)/shard_map/jit(_take)/gather | solution.py:128
  129.5 4.6 select_bitcast_fusion
  134.1 249.0 %while.16 = (s32[]{:T(128)}, f32[2,16,128]{2,1,0:T(8,128)}, f32[32]{0:T(128)S(1)}, bf16[2,2,32,128,128]{4,3,2,1,0:T(8,128)(2,1)}, s32[]{:T(128)}, /*index=5*/bf1...) while((s32[]{:T(128)}, f32[2,16,128]{2,1,0:T(8,128)}, ...), condition=%wide.region_8.9_spmd.clone, body=%wide.region_3.8_spmd.clone.sunk | while | flops 4459808768 | bytes 142112496 | solution.py:97
  148.4 2.6 fusion.413
  151.0 2.3 fusion.415
  153.3 2.3 fusion.414
  157.8 2.6 fusion.410
  160.4 2.3 fusion.416
  162.7 2.3 fusion.411
  173.2 2.6 fusion.427
  175.8 2.3 fusion.429
  178.1 2.3 fusion.428
  182.5 2.6 fusion.424
  185.2 2.3 fusion.430
  187.5 2.3 fusion.425
  210.6 2.6 fusion.413
  215.5 2.3 fusion.414
  220.0 2.6 fusion.410
  222.7 2.3 fusion.416
  224.9 2.3 fusion.411
  235.4 2.6 fusion.427
  240.3 2.3 fusion.428
  244.8 2.6 fusion.424
  249.7 2.3 fusion.425
  272.9 2.6 fusion.413
  277.8 2.3 fusion.414
  282.3 2.6 fusion.410
  284.9 2.3 fusion.416
  287.2 2.3 fusion.411
  297.6 2.6 fusion.427
  302.5 2.3 fusion.428
  307.0 2.6 fusion.424
  311.9 2.3 fusion.425
  335.1 2.6 fusion.413
  340.0 2.3 fusion.414
  344.5 2.6 fusion.410
  347.2 2.3 fusion.416
  349.4 2.3 fusion.411
  359.9 2.6 fusion.427
  364.8 2.3 fusion.428
  369.3 2.6 fusion.424
  374.2 2.3 fusion.425
  383.1 58.1 %psum.7 = f32[2,16,128]{2,1,0:T(8,128)S(1)} all-reduce(f32[2,16,128]{2,1,0:T(8,128)} %get-tuple-element.204), channel_id=1, replica_groups=mesh['tm'=16,'orb'=8] {'tm'}, use_global_device_ids=true, to_apply=%region_9.10 | all-reduce | flops 4096 | bytes 32768 | tf_op jit(solution)/shard_map/psum | solution.py:132
  441.1 28.1 %all_gather.7 = f32[2,128,128]{2,1,0:T(8,128)S(1)} all-gather(f32[2,16,128]{2,1,0:T(8,128)S(1)} %psum.7), channel_id=1, replica_groups=mesh['tm'=16,'orb'=8] {'orb'}, dimensions={1}, use_global_device_ids=true | all-gather | bytes 147456 | tf_op jit(solution)/shard_map/all_gather | solution.py:133
  (271 shorter events, 168.0 us)
Async XLA Ops:
  6.5 2.5 copy-start
  6.5 43.6 %all-gather.2.cloned.1.call-start = ((), (), s32[]{:S(2)}) async-start(), calls=%async_computation.1 | async-start | bytes 4718592 | tf_op jit(solution)/shard_map/all_gather | solution.py:126
  10.6 46.1 %copy-start.11 = (s32[512]{0:T(512)S(1)}, s32[512]{0:T(512)}, u32[]{:S(2)}) copy-start(s32[512]{0:T(512)} %param.11) | copy-start | bytes 6148
  50.1 69.5 %all-to-all-start = ((bf16[2,2,32,128,128]{4,3,1,0,2:T(8,128)(2,1)}), bf16[2,2,32,128,128]{4,3,1,0,2:T(8,128)(2,1)}, u32[]{:S(2)}, u32[]{:S(2)}) async-start(bf16[2,2,32,128,128]{4,3,1,0,2:T(8,128)(2,1)} %all-gather.2.cloned.1.call-done), calls=%async_computation | async-start | bytes 8388608 | tf_op jit(solution)/shard_map/all_to_all | solution.py:127
  57.9 1.1 copy-start.9
  58.0 1.2 copy-start.10
  58.0 3.1 copy-start.8
  134.1 0.5 copy-start.12
  134.1 6.7 %copy-start.2 = (bf16[128,128]{1,0:T(8,128)(2,1)}, bf16[128,128]{1,0:T(8,128)(2,1)S(1)}, u32[]{:S(2)}) copy-start(bf16[128,128]{1,0:T(8,128)(2,1)S(1)} %get-tuple-element.394) | copy-start | bytes 98308 | tf_op jit(solution)/shard_map/while
  160.4 4.5 copy-start.5
  185.2 4.5 copy-start.3
  185.2 4.5 copy-start.4
  187.5 8.3 %copy-start.6 = (f32[2,16,128]{2,1,0:T(8,128)S(1)}, f32[2,16,128]{2,1,0:T(8,128)}, u32[]{:S(2)}) copy-start(f32[2,16,128]{2,1,0:T(8,128)} %get-tuple-element.375) | copy-start | bytes 49156 | tf_op jit(solution)/shard_map/while
  187.5 8.9 %copy-start.13 = (f32[32]{0:T(128)S(1)}, f32[32]{0:T(128)}, u32[]{:S(2)}) copy-start(f32[32]{0:T(128)} %copy-done.12) | copy-start | bytes 388 | tf_op jit(solution)/shard_map/while
  195.7 0.6 copy-start.7
  196.4 0.5 copy-start.12
  196.4 6.7 %copy-start.2 = (bf16[128,128]{1,0:T(8,128)(2,1)}, bf16[128,128]{1,0:T(8,128)(2,1)S(1)}, u32[]{:S(2)}) copy-start(bf16[128,128]{1,0:T(8,128)(2,1)S(1)} %get-tuple-element.394) | copy-start | bytes 98308 | tf_op jit(solution)/shard_map/while
  222.7 4.5 copy-start.5
  247.4 4.5 copy-start.3
  247.4 4.5 copy-start.4
  249.7 8.3 %copy-start.6 = (f32[2,16,128]{2,1,0:T(8,128)S(1)}, f32[2,16,128]{2,1,0:T(8,128)}, u32[]{:S(2)}) copy-start(f32[2,16,128]{2,1,0:T(8,128)} %get-tuple-element.375) | copy-start | bytes 49156 | tf_op jit(solution)/shard_map/while
  249.7 8.9 %copy-start.13 = (f32[32]{0:T(128)S(1)}, f32[32]{0:T(128)}, u32[]{:S(2)}) copy-start(f32[32]{0:T(128)} %copy-done.12) | copy-start | bytes 388 | tf_op jit(solution)/shard_map/while
  258.0 0.6 copy-start.7
  258.6 0.5 copy-start.12
  258.6 6.7 %copy-start.2 = (bf16[128,128]{1,0:T(8,128)(2,1)}, bf16[128,128]{1,0:T(8,128)(2,1)S(1)}, u32[]{:S(2)}) copy-start(bf16[128,128]{1,0:T(8,128)(2,1)S(1)} %get-tuple-element.394) | copy-start | bytes 98308 | tf_op jit(solution)/shard_map/while
  284.9 4.5 copy-start.5
  309.7 4.5 copy-start.3
  309.7 4.5 copy-start.4
  311.9 8.3 %copy-start.6 = (f32[2,16,128]{2,1,0:T(8,128)S(1)}, f32[2,16,128]{2,1,0:T(8,128)}, u32[]{:S(2)}) copy-start(f32[2,16,128]{2,1,0:T(8,128)} %get-tuple-element.375) | copy-start | bytes 49156 | tf_op jit(solution)/shard_map/while
  311.9 8.9 %copy-start.13 = (f32[32]{0:T(128)S(1)}, f32[32]{0:T(128)}, u32[]{:S(2)}) copy-start(f32[32]{0:T(128)} %copy-done.12) | copy-start | bytes 388 | tf_op jit(solution)/shard_map/while
  320.2 0.6 copy-start.7
  320.8 0.5 copy-start.12
  320.8 6.7 %copy-start.2 = (bf16[128,128]{1,0:T(8,128)(2,1)}, bf16[128,128]{1,0:T(8,128)(2,1)S(1)}, u32[]{:S(2)}) copy-start(bf16[128,128]{1,0:T(8,128)(2,1)S(1)} %get-tuple-element.394) | copy-start | bytes 98308 | tf_op jit(solution)/shard_map/while
  347.1 4.5 copy-start.5
  371.9 4.5 copy-start.3
  371.9 4.5 copy-start.4
  374.2 8.3 %copy-start.6 = (f32[2,16,128]{2,1,0:T(8,128)S(1)}, f32[2,16,128]{2,1,0:T(8,128)}, u32[]{:S(2)}) copy-start(f32[2,16,128]{2,1,0:T(8,128)} %get-tuple-element.375) | copy-start | bytes 49156 | tf_op jit(solution)/shard_map/while
  374.2 8.9 %copy-start.13 = (f32[32]{0:T(128)S(1)}, f32[32]{0:T(128)}, u32[]{:S(2)}) copy-start(f32[32]{0:T(128)} %copy-done.12) | copy-start | bytes 388 | tf_op jit(solution)/shard_map/while
  382.5 0.6 copy-start.7
  383.1 89.1 %copy-start.1 = (bf16[2,2,32,16,128]{4,3,2,1,0:T(8,128)(2,1)S(1)}, bf16[2,2,32,16,128]{4,3,2,1,0:T(8,128)(2,1)}, u32[]{:S(2)}) copy-start(bf16[2,2,32,16,128]{4,3,2,1,0:T(8,128)(2,1)} %param.10) | copy-start | bytes 1572868
Sparse Core Ops, SparseCore 0:
  10.7 39.3 all-gather.1
where the time goes:
time: 482 us; the launch traced here: 479 us
  matrix products  219 us (45%)
  waiting for transfers between devices  95.1 us (20%)
  blocking collectives  86.2 us (18%)
  local copies, waits for them, and re-layouts  46.3 us (10%)
  between operations  13.6 us (3%)
  other arithmetic  11.6 us (2%)
  starting transfers between devices  6.58 us (1%)
    psum x1, blocking collectives, on_device(): summed_rows = lax.psum(local_collision, 'tm')  58.1 us
    all_to_all x1, waiting for transfers between devices, on_device(): lax.all_to_all(full_sorted, 'tm', split_axis=2, concat_axis=2, tiled=True)  55.6 us
    dot_general x24, matrix products, complex_einsum(): jnp.einsum(form, left_re, right_im, preferred_element_type=jnp.float32)  48.3 us
    dot_general x24, matrix products, complex_einsum(): jnp.einsum(form, left_im, right_im, preferred_element_type=jnp.float32)  48.2 us
    dot_general x24, matrix products, complex_einsum(): jnp.einsum(form, left_im, right_re, preferred_element_type=jnp.float32)  45 us
    dot_general x24, matrix products, complex_einsum(): jnp.einsum(form, left_re, right_re, preferred_element_type=jnp.float32)  44.8 us
    all_gather x1, waiting for transfers between devices, on_device(): full_sorted = lax.all_gather(sorted_slab, 'orb', axis=3, tiled=True)  39.5 us
    all_gather x1, blocking collectives, on_device(): collision = lax.all_gather(summed_rows, 'orb', axis=1, tiled=True)  28.1 us
  transfers between devices with their start and end apart: 2, of which 2 were waited for; matrix products, arithmetic and copies ran while one was open for 1% of the time, Pallas kernels for 0%

commit v1 on v0

--- a/solution.py
+++ b/solution.py
@@ -129,7 +129,7 @@
     local_collision = history_terms(
         forward, back_full, weights, interaction, inter_rows, row_start, row_count
     )
-    summed_rows = lax.psum(local_collision, "tm")
+    summed_rows = jnp.sum(lax.all_gather(local_collision, "tm"), axis=0)
     collision = lax.all_gather(summed_rows, "orb", axis=1, tiled=True)
     own_rows = lax.dynamic_slice_in_dim(collision, row_start, row_count, 1)
     own_columns = lax.dynamic_slice_in_dim(collision, row_start, row_count, 2)

time: 482 us -> 433 us (0.90)
  blocking collectives: 86.2 us -> 36.8 us
    psum x1 -> x0, blocking collectives: 58.1 us -> none  [on_device(): summed_rows = lax.psum(local_collision, 'tm')]
    all_gather x0 -> x1, blocking collectives: none -> 17.6 us  [on_device(): summed_rows = jnp.sum(lax.all_gather(local_collision, 'tm'), axis=0)]
    all_gather x1, blocking collectives: 28.1 us -> 19.2 us  [on_device(): collision = lax.all_gather(summed_rows, 'orb', axis=1, tiled=True)]
  transfers between devices with their start and end apart: 2 -> 2, of which waited for: 2 -> 2; matrix products, arithmetic and copies ran while one was open for 1% -> 2% of each run, Pallas kernels for 0% -> 0%
where the time goes in v1:
time: 433 us; the launch traced here: 430 us
  matrix products  219 us (51%)
  waiting for transfers between devices  95.1 us (22%)
  local copies, waits for them, and re-layouts  46.3 us (11%)
  blocking collectives  36.8 us (8%)
  between operations  13.6 us (3%)
  other arithmetic  11.6 us (3%)
  starting transfers between devices  6.58 us (2%)
    all_to_all x1, waiting for transfers between devices, on_device(): lax.all_to_all(full_sorted, 'tm', split_axis=2, concat_axis=2, tiled=True)  55.6 us
    dot_general x24, matrix products, complex_einsum(): jnp.einsum(form, left_re, right_im, preferred_element_type=jnp.float32)  48.3 us
    dot_general x24, matrix products, complex_einsum(): jnp.einsum(form, left_im, right_im, preferred_element_type=jnp.float32)  48.2 us
    dot_general x24, matrix products, complex_einsum(): jnp.einsum(form, left_im, right_re, preferred_element_type=jnp.float32)  45 us
    dot_general x24, matrix products, complex_einsum(): jnp.einsum(form, left_re, right_re, preferred_element_type=jnp.float32)  44.8 us
    all_gather x1, waiting for transfers between devices, on_device(): full_sorted = lax.all_gather(sorted_slab, 'orb', axis=3, tiled=True)  39.5 us
    all_gather x1, blocking collectives, on_device(): collision = lax.all_gather(summed_rows, 'orb', axis=1, tiled=True)  19.2 us
    all_gather x1, blocking collectives, on_device(): summed_rows = jnp.sum(lax.all_gather(local_collision, 'tm'), axis=0)  17.6 us
  transfers between devices with their start and end apart: 2, of which 2 were waited for; matrix products, arithmetic and copies ran while one was open for 2% of the time, Pallas kernels for 0%

profile of v1, /device:TPU:1, one launch (start us, length us, event | category | flops | bytes accessed | tf_op | source)
XLA Modules:
  0.0 429.7 jit_solution(7471554814628150537)
XLA Ops:
  10.6 39.5 %all-gather.3.cloned.1.call-done = bf16[2,2,32,128,128]{4,3,1,0,2:T(8,128)(2,1)} async-done(((bf16[2,2,32,16,128]{4,3,1,0,2:T(8,128)(2,1)}), bf16[2,2,32,128,128]{4,3,1,0,2:T(8,128)(2,1)}) %all-gather.3.cloned.1.call-update) | async-done | bytes 4194320 | tf_op jit(solution)/shard_map/all_gather | solution.py:126
  50.1 6.6 %all-to-all-start = ((bf16[2,2,32,128,128]{4,3,1,0,2:T(8,128)(2,1)}), bf16[2,2,32,128,128]{4,3,1,0,2:T(8,128)(2,1)}, u32[]{:S(2)}, u32[]{:S(2)}) async-start(bf16[2,2,32,128,128]{4,3,1,0,2:T(8,128)(2,1)} %all-gather.3.cloned.1.call-done), calls=%async_computation | async-start | bytes 8388608 | tf_op jit(solution)/shard_map/all_to_all | solution.py:127
  64.0 55.6 %all-to-all-done = bf16[2,2,32,128,128]{4,3,1,0,2:T(8,128)(2,1)} async-done(((bf16[2,2,32,128,128]{4,3,1,0,2:T(8,128)(2,1)}), bf16[2,2,32,128,128]{4,3,1,0,2:T(8,128)(2,1)}, u32[]{:S(2)}, u32[]{:S(2)}) %all-to-all-start) | async-done | bytes 4194336 | tf_op jit(solution)/shard_map/all_to_all | solution.py:127
  119.6 4.7 %copy.65 = bf16[2,2,32,128,128]{4,3,2,1,0:T(8,128)(2,1)} copy(bf16[2,2,32,128,128]{4,3,1,0,2:T(8,128)(2,1)} %all-to-all-done) | data formatting | bytes 8388608 | tf_op jit(solution)/shard_map/all_to_all | solution.py:127
  124.3 5.2 %gather_fusion.1 = bf16[32,2,2,128,128]{4,3,2,1,0:T(8,128)(2,1)} fusion(bf16[2,2,32,128,128]{4,3,2,1,0:T(8,128)(2,1)} %copy.65, s32[1024]{0:T(1024)S(1)} %pad_clamp_fusion), kind=kCustom, calls=%fused_computation.1 | custom fusion | bytes 8388736 | tf_op jit(solution)/shard_map/jit(_take)/gather | solution.py:128
  129.5 4.6 %select_bitcast_fusion = bf16[2,2,32,128,128]{4,3,1,0,2:T(8,128)(2,1)} fusion(bf16[32,2,2,128,128]{4,3,2,1,0:T(8,128)(2,1)} %gather_fusion.1, pred[32]{0:T(512)(128)(4,1)S(1)} %compare_and_fusion.1), kind=kLoop, calls=%fused_computation.226 | loop fusion | flops 2097152 | bytes 8388640 | tf_op jit(solution)/shard_map/jit(_take)/select_n | solution.py:128
  134.1 249.0 %while.16 = (s32[]{:T(128)}, f32[2,16,128]{2,1,0:T(8,128)}, f32[32]{0:T(128)S(1)}, bf16[2,2,32,128,128]{4,3,2,1,0:T(8,128)(2,1)}, s32[]{:T(128)}, /*index=5*/bf1...) while((s32[]{:T(128)}, f32[2,16,128]{2,1,0:T(8,128)}, ...), condition=%wide.region_8.9_spmd.clone, body=%wide.region_3.8_spmd.clone.sunk | while | flops 4459808768 | bytes 142112496 | solution.py:97
  148.4 2.6 fusion.413
  151.0 2.3 fusion.415
  153.3 2.3 fusion.414
  157.8 2.6 fusion.410
  160.4 2.3 fusion.416
  162.7 2.3 fusion.411
  173.2 2.6 fusion.427
  175.8 2.3 fusion.429
  178.1 2.3 fusion.428
  182.5 2.6 fusion.424
  185.2 2.3 fusion.430
  187.5 2.3 fusion.425
  210.6 2.6 fusion.413
  215.5 2.3 fusion.414
  220.0 2.6 fusion.410
  222.7 2.3 fusion.416
  224.9 2.3 fusion.411
  235.4 2.6 fusion.427
  240.3 2.3 fusion.428
  244.8 2.6 fusion.424
  249.7 2.3 fusion.425
  272.9 2.6 fusion.413
  277.8 2.3 fusion.414
  282.3 2.6 fusion.410
  284.9 2.3 fusion.416
  287.2 2.3 fusion.411
  297.6 2.6 fusion.427
  302.5 2.3 fusion.428
  307.0 2.6 fusion.424
  311.9 2.3 fusion.425
  335.1 2.6 fusion.413
  340.0 2.3 fusion.414
  344.5 2.6 fusion.410
  347.2 2.3 fusion.416
  349.4 2.3 fusion.411
  359.9 2.6 fusion.427
  364.8 2.3 fusion.428
  369.3 2.6 fusion.424
  374.2 2.3 fusion.425
  383.1 17.6 %all-gather = f32[32,16,128]{2,1,0:T(8,128)S(1)} all-gather(f32[2,16,128]{2,1,0:T(8,128)} %get-tuple-element.204), channel_id=2, replica_groups=mesh['tm'=16,'orb'=8] {'tm'}, dimensions={0}, use_global_device_ids=true | all-gather | bytes 278528 | tf_op jit(solution)/shard_map/all_gather | solution.py:132
  400.7 19.2 %all_gather.15 = f32[2,128,128]{2,1,0:T(8,128)S(1)} all-gather(f32[2,16,128]{2,1,0:T(8,128)S(1)} %reduce_sum.69), channel_id=1, replica_groups=mesh['tm'=16,'orb'=8] {'orb'}, dimensions={1}, use_global_device_ids=true | all-gather | bytes 147456 | tf_op jit(solution)/shard_map/all_gather | solution.py:133
  (272 shorter events, 168.0 us)
Async XLA Ops:
  6.5 2.5 copy-start
  6.5 43.6 %all-gather.3.cloned.1.call-start = ((), (), s32[]{:S(2)}) async-start(), calls=%async_computation.1 | async-start | bytes 4718592 | tf_op jit(solution)/shard_map/all_gather | solution.py:126
  10.6 46.1 %copy-start.11 = (s32[512]{0:T(512)S(1)}, s32[512]{0:T(512)}, u32[]{:S(2)}) copy-start(s32[512]{0:T(512)} %param.11) | copy-start | bytes 6148
  50.1 69.5 %all-to-all-start = ((bf16[2,2,32,128,128]{4,3,1,0,2:T(8,128)(2,1)}), bf16[2,2,32,128,128]{4,3,1,0,2:T(8,128)(2,1)}, u32[]{:S(2)}, u32[]{:S(2)}) async-start(bf16[2,2,32,128,128]{4,3,1,0,2:T(8,128)(2,1)} %all-gather.3.cloned.1.call-done), calls=%async_computation | async-start | bytes 8388608 | tf_op jit(solution)/shard_map/all_to_all | solution.py:127
  57.9 1.1 copy-start.9
  58.0 1.2 copy-start.10
  58.0 3.1 copy-start.8
  134.1 0.5 copy-start.12
  134.1 6.7 %copy-start.2 = (bf16[128,128]{1,0:T(8,128)(2,1)}, bf16[128,128]{1,0:T(8,128)(2,1)S(1)}, u32[]{:S(2)}) copy-start(bf16[128,128]{1,0:T(8,128)(2,1)S(1)} %get-tuple-element.402) | copy-start | bytes 98308 | tf_op jit(solution)/shard_map/while
  160.4 4.5 %copy-start.5 = (f32[8,16,128]{2,1,0:T(8,128)S(1)}, f32[8,16,128]{2,1,0:T(8,128)}, u32[]{:S(2)}) copy-start(f32[8,16,128]{2,1,0:T(8,128)} %fusion.408) | copy-start | bytes 196612 | tf_op jit(solution)/shard_map/while
  185.2 4.5 %copy-start.3 = (bf16[128,128]{1,0:T(8,128)(2,1)S(1)}, bf16[128,128]{1,0:T(8,128)(2,1)}, u32[]{:S(2)}) copy-start(bf16[128,128]{1,0:T(8,128)(2,1)} %copy-done.2) | copy-start | bytes 98308 | tf_op jit(solution)/shard_map/while
  185.2 4.5 %copy-start.4 = (f32[8,16,128]{2,1,0:T(8,128)S(1)}, f32[8,16,128]{2,1,0:T(8,128)}, u32[]{:S(2)}) copy-start(f32[8,16,128]{2,1,0:T(8,128)} %fusion.422) | copy-start | bytes 196612 | tf_op jit(solution)/shard_map/while
  187.5 8.3 %copy-start.6 = (f32[2,16,128]{2,1,0:T(8,128)S(1)}, f32[2,16,128]{2,1,0:T(8,128)}, u32[]{:S(2)}) copy-start(f32[2,16,128]{2,1,0:T(8,128)} %get-tuple-element.383) | copy-start | bytes 49156 | tf_op jit(solution)/shard_map/while
  187.5 8.9 %copy-start.13 = (f32[32]{0:T(128)S(1)}, f32[32]{0:T(128)}, u32[]{:S(2)}) copy-start(f32[32]{0:T(128)} %copy-done.12) | copy-start | bytes 388 | tf_op jit(solution)/shard_map/while
  195.7 0.6 copy-start.7
  196.4 0.5 copy-start.12
  196.4 6.7 %copy-start.2 = (bf16[128,128]{1,0:T(8,128)(2,1)}, bf16[128,128]{1,0:T(8,128)(2,1)S(1)}, u32[]{:S(2)}) copy-start(bf16[128,128]{1,0:T(8,128)(2,1)S(1)} %get-tuple-element.402) | copy-start | bytes 98308 | tf_op jit(solution)/shard_map/while
  222.7 4.5 %copy-start.5 = (f32[8,16,128]{2,1,0:T(8,128)S(1)}, f32[8,16,128]{2,1,0:T(8,128)}, u32[]{:S(2)}) copy-start(f32[8,16,128]{2,1,0:T(8,128)} %fusion.408) | copy-start | bytes 196612 | tf_op jit(solution)/shard_map/while
  247.4 4.5 %copy-start.3 = (bf16[128,128]{1,0:T(8,128)(2,1)S(1)}, bf16[128,128]{1,0:T(8,128)(2,1)}, u32[]{:S(2)}) copy-start(bf16[128,128]{1,0:T(8,128)(2,1)} %copy-done.2) | copy-start | bytes 98308 | tf_op jit(solution)/shard_map/while
  247.4 4.5 %copy-start.4 = (f32[8,16,128]{2,1,0:T(8,128)S(1)}, f32[8,16,128]{2,1,0:T(8,128)}, u32[]{:S(2)}) copy-start(f32[8,16,128]{2,1,0:T(8,128)} %fusion.422) | copy-start | bytes 196612 | tf_op jit(solution)/shard_map/while
  249.7 8.3 %copy-start.6 = (f32[2,16,128]{2,1,0:T(8,128)S(1)}, f32[2,16,128]{2,1,0:T(8,128)}, u32[]{:S(2)}) copy-start(f32[2,16,128]{2,1,0:T(8,128)} %get-tuple-element.383) | copy-start | bytes 49156 | tf_op jit(solution)/shard_map/while
  249.7 8.9 %copy-start.13 = (f32[32]{0:T(128)S(1)}, f32[32]{0:T(128)}, u32[]{:S(2)}) copy-start(f32[32]{0:T(128)} %copy-done.12) | copy-start | bytes 388 | tf_op jit(solution)/shard_map/while
  258.0 0.6 copy-start.7
  258.6 0.5 copy-start.12
  258.6 6.7 %copy-start.2 = (bf16[128,128]{1,0:T(8,128)(2,1)}, bf16[128,128]{1,0:T(8,128)(2,1)S(1)}, u32[]{:S(2)}) copy-start(bf16[128,128]{1,0:T(8,128)(2,1)S(1)} %get-tuple-element.402) | copy-start | bytes 98308 | tf_op jit(solution)/shard_map/while
  284.9 4.5 %copy-start.5 = (f32[8,16,128]{2,1,0:T(8,128)S(1)}, f32[8,16,128]{2,1,0:T(8,128)}, u32[]{:S(2)}) copy-start(f32[8,16,128]{2,1,0:T(8,128)} %fusion.408) | copy-start | bytes 196612 | tf_op jit(solution)/shard_map/while
  309.7 4.5 %copy-start.3 = (bf16[128,128]{1,0:T(8,128)(2,1)S(1)}, bf16[128,128]{1,0:T(8,128)(2,1)}, u32[]{:S(2)}) copy-start(bf16[128,128]{1,0:T(8,128)(2,1)} %copy-done.2) | copy-start | bytes 98308 | tf_op jit(solution)/shard_map/while
  309.7 4.5 %copy-start.4 = (f32[8,16,128]{2,1,0:T(8,128)S(1)}, f32[8,16,128]{2,1,0:T(8,128)}, u32[]{:S(2)}) copy-start(f32[8,16,128]{2,1,0:T(8,128)} %fusion.422) | copy-start | bytes 196612 | tf_op jit(solution)/shard_map/while
  311.9 8.3 %copy-start.6 = (f32[2,16,128]{2,1,0:T(8,128)S(1)}, f32[2,16,128]{2,1,0:T(8,128)}, u32[]{:S(2)}) copy-start(f32[2,16,128]{2,1,0:T(8,128)} %get-tuple-element.383) | copy-start | bytes 49156 | tf_op jit(solution)/shard_map/while
  311.9 8.9 %copy-start.13 = (f32[32]{0:T(128)S(1)}, f32[32]{0:T(128)}, u32[]{:S(2)}) copy-start(f32[32]{0:T(128)} %copy-done.12) | copy-start | bytes 388 | tf_op jit(solution)/shard_map/while
  320.2 0.6 copy-start.7
  320.8 0.5 copy-start.12
  320.8 6.7 %copy-start.2 = (bf16[128,128]{1,0:T(8,128)(2,1)}, bf16[128,128]{1,0:T(8,128)(2,1)S(1)}, u32[]{:S(2)}) copy-start(bf16[128,128]{1,0:T(8,128)(2,1)S(1)} %get-tuple-element.402) | copy-start | bytes 98308 | tf_op jit(solution)/shard_map/while
  347.1 4.5 %copy-start.5 = (f32[8,16,128]{2,1,0:T(8,128)S(1)}, f32[8,16,128]{2,1,0:T(8,128)}, u32[]{:S(2)}) copy-start(f32[8,16,128]{2,1,0:T(8,128)} %fusion.408) | copy-start | bytes 196612 | tf_op jit(solution)/shard_map/while
  371.9 4.5 %copy-start.3 = (bf16[128,128]{1,0:T(8,128)(2,1)S(1)}, bf16[128,128]{1,0:T(8,128)(2,1)}, u32[]{:S(2)}) copy-start(bf16[128,128]{1,0:T(8,128)(2,1)} %copy-done.2) | copy-start | bytes 98308 | tf_op jit(solution)/shard_map/while
  371.9 4.5 %copy-start.4 = (f32[8,16,128]{2,1,0:T(8,128)S(1)}, f32[8,16,128]{2,1,0:T(8,128)}, u32[]{:S(2)}) copy-start(f32[8,16,128]{2,1,0:T(8,128)} %fusion.422) | copy-start | bytes 196612 | tf_op jit(solution)/shard_map/while
  374.2 8.3 %copy-start.6 = (f32[2,16,128]{2,1,0:T(8,128)S(1)}, f32[2,16,128]{2,1,0:T(8,128)}, u32[]{:S(2)}) copy-start(f32[2,16,128]{2,1,0:T(8,128)} %get-tuple-element.383) | copy-start | bytes 49156 | tf_op jit(solution)/shard_map/while
  374.2 8.9 %copy-start.13 = (f32[32]{0:T(128)S(1)}, f32[32]{0:T(128)}, u32[]{:S(2)}) copy-start(f32[32]{0:T(128)} %copy-done.12) | copy-start | bytes 388 | tf_op jit(solution)/shard_map/while
  382.5 0.6 copy-start.7
  383.1 39.8 %copy-start.1 = (bf16[2,2,32,16,128]{4,3,2,1,0:T(8,128)(2,1)S(1)}, bf16[2,2,32,16,128]{4,3,2,1,0:T(8,128)(2,1)}, u32[]{:S(2)}) copy-start(bf16[2,2,32,16,128]{4,3,2,1,0:T(8,128)(2,1)} %param.10) | copy-start | bytes 1572868
Sparse Core Ops, SparseCore 0:
  10.7 39.3 all-gather.2
